TPU v7x, 32 devices: a whole 2x2x4 slice. The times are simulated.
32 devices in a mesh: blk: 8 (over z, y), hid: 4 (over x, core).
Axes of the slice: x: 2, y: 2, z: 4, core: 2. Of those that a mesh axis runs over, the one named last changes fastest.
Arguments:
- queries: bfloat16 [768, 128], P('blk'), may hold values from -6 to 6
- node_table: bfloat16 [65536, 128], P('blk'), may hold values from -6 to 6
- beam: int32 [768, 128], P('blk'), may hold values from 0 to 65535, as said below
- w_query: bfloat16 [128, 256], P(None, 'hid'), may hold values from -0.5 to 0.5
- w_node: bfloat16 [128, 256], P(None, 'hid'), may hold values from -0.5 to 0.5
- w_cross: bfloat16 [128, 256], P(None, 'hid'), may hold values from -0.5 to 0.5
- bias_hidden: bfloat16 [256], P('hid'), may hold values from -3 to 3
- w_out: bfloat16 [256], P('hid'), may hold values from -0.375 to 0.375
Outputs:
- scores: float32 [768, 128], P('blk', 'hid')
Inputs may be any that keep to these rules, and one draw needn't show every extreme that they name: `beam`: each query's entries are distinct and come in sibling pairs 2p, 2p + 1 of 64 parents. Among the rows of one blk index (96 queries) at most 3072 entries lie in any one aligned range of 8192 nodes, and some range holds exactly 3072.
All inputs are finite; a program needn't handle non-finite values.
Results may differ from a plain program's by a relative error of at most 0.007.
Values may be sent and summed in bfloat16 or wider, within the bound.
No kernel may reach another device: no remote copies, remote signals or barrier semaphores. Data moves between devices by JAX's collectives and lax.ppermute only.
A program may use at most 64 MiB of HBM per device.

v0:
```python
import functools

import jax
import jax.numpy as jnp
from jax import lax
from jax.experimental import pallas as pl
from jax.experimental.pallas import tpu as pltpu
from jax.sharding import PartitionSpec as P


SLOT = 8
KIDS = 2 * SLOT
READY = 2
FIELD = 20
SHIFT = 8
LANES = 128
SUBLANES = 8
STATIC = 2

VMEM = pl.BlockSpec(memory_space=pltpu.VMEM)


def pack_kernel(digits, *refs):
    sources, (message_ref, pack_ref), held, done = refs[:7], refs[7:9], refs[9:-1], refs[-1]
    copies = [
        pltpu.make_async_copy(source, target, done.at[i])
        for i, (source, target) in enumerate(zip(sources, held))
    ]
    for copy in copies:
        copy.start()
    beam_ref, query_ref = held[:2]
    weights, (out_row, bias_row) = held[2:5], held[5:7]
    rows = beam_ref.shape[0]
    part = weights[0].shape[0]
    width = pack_ref.shape[1]
    for copy in copies:
        copy.wait()
    ids = beam_ref[...]
    for d in range(digits):
        digit = (ids >> (SHIFT * (digits - 1 - d))) & (2**SHIFT - 1)
        message_ref[(d + 1) * rows : (d + 2) * rows, :] = digit.astype(jnp.float32).astype(
            jnp.bfloat16
        )
    message_ref[0:rows, :] = query_ref[...]
    for i, weight in enumerate(weights):
        pack_ref[i * part : (i + 1) * part, :] = weight[...]
    tail = pack_ref.shape[0] - 3 * part
    ends = jnp.concatenate(
        [
            out_row[...].astype(jnp.float32),
            bias_row[...].astype(jnp.float32),
            jnp.zeros((tail - 2, part), jnp.float32),
        ],
        axis=0,
    )
    ends = jnp.concatenate([ends, jnp.zeros((tail, width - part), jnp.float32)], axis=1)
    pack_ref[3 * part :, :] = ends.astype(jnp.bfloat16)


def pack(queries, beam, digits, weights, w_out, bias):
    rows, width = queries.shape
    part = w_out.shape[0]
    given = (beam, queries, *[w.T for w in weights], w_out[None, :], bias[None, :])
    return pl.pallas_call(
        functools.partial(pack_kernel, digits),
        in_specs=[pl.BlockSpec(memory_space=pltpu.HBM)] * len(given),
        out_specs=(VMEM, VMEM),
        out_shape=(
            jax.ShapeDtypeStruct(((digits + 1) * rows, width), jnp.bfloat16),
            jax.ShapeDtypeStruct((3 * part + 16, width), jnp.bfloat16),
        ),
        scratch_shapes=[pltpu.VMEM(x.shape, x.dtype) for x in given]
        + [pltpu.SemaphoreType.DMA((len(given),))],
        compiler_params=pltpu.CompilerParams(vmem_limit_bytes=60 * 2**20),
    )(*given)


def widen_kernel(chunks, table_ref, wide_ref, held_ref, done):
    rows = table_ref.shape[0] // chunks
    copies = [
        pltpu.make_async_copy(
            table_ref.at[pl.ds(i * rows, rows)], held_ref.at[pl.ds(i * rows, rows)], done.at[i]
        )
        for i in range(chunks)
    ]
    for copy in copies:
        copy.start()
    for i, copy in enumerate(copies):
        copy.wait()
        some = slice(i * rows, (i + 1) * rows)
        wide_ref[some, :] = held_ref[some, :].astype(jnp.float32)


def widen(table):
    rows, width = table.shape
    chunks = 8
    return pl.pallas_call(
        functools.partial(widen_kernel, chunks),
        in_specs=[pl.BlockSpec(memory_space=pltpu.HBM)],
        out_specs=VMEM,
        out_shape=jax.ShapeDtypeStruct((rows, width), jnp.float32),
        scratch_shapes=[pltpu.VMEM((rows, width), table.dtype), pltpu.SemaphoreType.DMA((chunks,))],
        compiler_params=pltpu.CompilerParams(vmem_limit_bytes=12 * 2**20),
        cost_estimate=pl.CostEstimate(flops=0, bytes_accessed=6 * rows * width, transcendentals=0),
    )(table)


def score_kernel(shard_rows, digits, turns, parts, tile_queries, *refs):
    asked, table_ref, packs = refs[:turns], refs[turns], refs[turns + 1 : turns + 1 + parts]
    outs = refs[turns + 1 + parts : 2 * turns + 1 + parts]
    (
        mix_ref,
        out_row_ref,
        sum_ref,
        query_ref,
        start_ref,
        key_ref,
        need_ref,
        flat_ref,
        total_ref,
        found_ref,
        place_ref,
        passes_ref,
        done,
    ) = refs[2 * turns + 1 + parts :]
    width, rows = outs[0].shape
    feat = table_ref.shape[1]
    hidden_width = mix_ref.shape[1]
    part = hidden_width // parts
    tile = tile_queries * KIDS
    tiles = rows // tile_queries
    limit = width // 2 // SLOT

    ids = jnp.concatenate([a[rows : 2 * rows, :] for a in asked], axis=0).astype(jnp.int32)
    for d in range(2, digits + 1):
        digit = jnp.concatenate([a[d * rows : (d + 1) * rows, :] for a in asked], axis=0)
        ids = (ids << SHIFT) + digit.astype(jnp.int32)
    local = ids - lax.axis_index("blk") * shard_rows
    owned = (local >= 0) & (local < shard_rows)
    even = owned & ((local & 1) == 0)
    lane = lax.broadcasted_iota(jnp.int32, (turns * rows, width), 1)
    earlier = (
        lax.broadcasted_iota(jnp.int32, (width, width), 0)
        < lax.broadcasted_iota(jnp.int32, (width, width), 1)
    ).astype(jnp.bfloat16)
    even_count = even.astype(jnp.float32)
    rank = jnp.dot(even_count.astype(jnp.bfloat16), earlier, preferred_element_type=jnp.float32)
    shift = lane - rank.astype(jnp.int32)
    word = jnp.where(even, (local >> 1) + (shift << FIELD) + (1 << (FIELD + 8)), 0)
    hop = 1
    while hop < width:
        bit = hop << FIELD
        moved = pltpu.roll(word, width - hop, 1)
        word = jnp.where((moved & bit) != 0, moved, jnp.where((word & bit) != 0, 0, word))
        hop *= 2
    front = word & ((1 << FIELD) - 1)
    ahead = []
    for j in range(turns):
        slots = (front[j * rows : (j + 1) * rows, :] * 2).T
        for c in range(limit):
            flat_ref[j * limit + c, :, 0:rows] = slots[c * SLOT : (c + 1) * SLOT, :]
        ahead.append(
            pltpu.make_async_copy(
                flat_ref.at[pl.ds(j * limit, READY)],
                place_ref.at[pl.ds(j * READY, READY)],
                done.at[j],
            )
        )
        ahead[-1].start()
        most = jnp.max(
            jnp.sum(even_count[j * rows : (j + 1) * rows, :], axis=1, keepdims=True)
        ).astype(jnp.int32)
        passes_ref[j] = (most + (SLOT - 1)) // SLOT
    need_ref[...] = jnp.where(word != 0, front, -1)
    key_ref[...] = jnp.where(owned, local, -4)

    stacked = [
        jnp.concatenate([p[i * part : (i + 1) * part, :] for p in packs], axis=0) for i in range(3)
    ]
    mix_ref[0:feat, :] = stacked[1].T
    mix_ref[feat:, :] = stacked[2].T
    ends = [p[3 * part :, :].astype(jnp.float32) for p in packs]
    out_row = jnp.concatenate([e[0:1, 0:part] for e in ends], axis=1)
    bias = jnp.concatenate([e[1:2, 0:part] for e in ends], axis=1)
    out_row_ref[...] = jnp.broadcast_to(out_row, out_row_ref.shape)
    queries = jnp.concatenate([a[0:rows, :] for a in asked], axis=0)
    query_ref[...] = queries.astype(jnp.float32)
    start_ref[...] = (
        jnp.dot(queries, stacked[0].T, preferred_element_type=jnp.float32) + bias
    )
    sum_ref[...] = (
        lax.broadcasted_iota(jnp.int32, (tile_queries, tile), 1) // KIDS
        == lax.broadcasted_iota(jnp.int32, (tile_queries, tile), 0)
    ).astype(jnp.bfloat16)
    total_ref[...] = jnp.zeros(total_ref.shape, jnp.float32)
    for copy in ahead:
        copy.wait()

    def gather(block, k):
        for i in range(tile_queries):
            for t in range(SLOT):
                at = pl.multiple_of(place_ref[block, t, k * tile_queries + i], 2)
                found_ref[k, pl.ds(i * KIDS + 2 * t, 2), :] = table_ref[pl.ds(at, 2), :]

    def queries_of(j, k):
        if isinstance(j, int):
            return slice(j * rows + k * tile_queries, j * rows + (k + 1) * tile_queries)
        return pl.ds(pl.multiple_of(j * rows + k * tile_queries, SUBLANES), tile_queries)

    def score(j, k):
        some = queries_of(j, k)
        nodes = found_ref[k]
        spread = jnp.broadcast_to(query_ref[some, :][:, None, :], (tile_queries, KIDS, feat))
        crossed = (nodes * spread.reshape(tile, feat)).astype(jnp.bfloat16)
        joined = jnp.concatenate([nodes.astype(jnp.bfloat16), crossed], axis=1)
        pre = jnp.dot(joined, mix_ref[...], preferred_element_type=jnp.float32)
        pre = pre.reshape(tile_queries, KIDS, hidden_width) + start_ref[some, :][:, None, :]
        weighed = jnp.maximum(pre.reshape(tile, hidden_width), 0.0) * out_row_ref[0:1, :]
        return jnp.sum(weighed, axis=1, keepdims=True)

    def settle(j, c, k, scores):
        some = queries_of(j, k)
        need = need_ref[some, :]
        if isinstance(c, int):
            need = need[:, c * SLOT : (c + 1) * SLOT]
        else:
            need = pltpu.roll(need, (width - c * SLOT) % width, 1)
        key = key_ref[some, :]
        above = key >> 1
        parity = key & 1
        code = jnp.full((tile_queries, width), -1, jnp.int32)
        for t in range(SLOT):
            code = jnp.where(above == need[:, t : t + 1], 2 * t + parity, code)
        slot = lax.broadcasted_iota(jnp.int32, (tile_queries, KIDS, width), 1)
        hits = jnp.where(code[:, None, :] == slot, scores.reshape(tile_queries, KIDS, 1), 0.0)
        total_ref[some, :] += jnp.dot(
            sum_ref[...],
            hits.reshape(tile, width).astype(jnp.bfloat16),
            preferred_element_type=jnp.float32,
        )

    def one_pass(j, c, block):
        gather(block, 0)
        before = None
        for k in range(tiles):
            if k + 1 < tiles:
                gather(block, k + 1)
            scores = score(j, k)
            if k > 0:
                settle(j, c, k - 1, before)
            before = scores
        settle(j, c, tiles - 1, before)

    def late_pass(j, c):
        copy = pltpu.make_async_copy(
            flat_ref.at[j * limit + c], place_ref.at[turns * READY], done.at[turns]
        )
        copy.start()
        copy.wait()
        one_pass(j, c, turns * READY)

    if turns <= STATIC:
        for j in range(turns):
            for c in range(READY):
                pl.when(passes_ref[j] > c)(functools.partial(one_pass, j, c, j * READY + c))

            def later(c, carry, j=j):
                late_pass(j, c)
                return carry

            lax.fori_loop(READY, passes_ref[j], later, 0)
    else:

        def one_source(j, carry):
            def every(c, inner):
                late_pass(j, c)
                return inner

            return lax.fori_loop(0, passes_ref[j], every, carry)

        lax.fori_loop(0, turns, one_source, 0)
    for j, out_ref in enumerate(outs):
        out_ref[...] = total_ref[j * rows : (j + 1) * rows, :].T.astype(out_ref.dtype)


def score_sources(asked, rows, shard_rows, wide, packs):
    turns = len(asked)
    feat = asked[0].shape[1]
    width = feat
    digits = asked[0].shape[0] // rows - 1
    part = (packs[0].shape[0] - 16) // 3
    hidden = part * len(packs)
    tile_queries = next(n for n in (48, 32, 24, 16, 8) if rows % n == 0)
    tile = tile_queries * KIDS
    lanes = -(-rows // LANES) * LANES
    count = turns * rows
    return pl.pallas_call(
        functools.partial(score_kernel, shard_rows, digits, turns, len(packs), tile_queries),
        in_specs=[VMEM] * (turns + 1 + len(packs)),
        out_specs=(VMEM,) * turns,
        out_shape=(jax.ShapeDtypeStruct((width, rows), jnp.bfloat16),) * turns,
        scratch_shapes=[
            pltpu.VMEM((2 * feat, hidden), jnp.bfloat16),
            pltpu.VMEM((SUBLANES, hidden), jnp.float32),
            pltpu.VMEM((tile_queries, tile), jnp.bfloat16),
            pltpu.VMEM((count, feat), jnp.float32),
            pltpu.VMEM((count, hidden), jnp.float32),
            pltpu.VMEM((count, width), jnp.int32),
            pltpu.VMEM((count, width), jnp.int32),
            pltpu.VMEM((turns * (width // 2 // SLOT), SLOT, lanes), jnp.int32),
            pltpu.VMEM((count, width), jnp.float32),
            pltpu.VMEM((rows // tile_queries, tile, feat), jnp.float32),
            pltpu.SMEM((turns * READY + 1, SLOT, lanes), jnp.int32),
            pltpu.SMEM((turns,), jnp.int32),
            pltpu.SemaphoreType.DMA((turns + 1,)),
        ],
        compiler_params=pltpu.CompilerParams(vmem_limit_bytes=16 * 2**20),
        cost_estimate=pl.CostEstimate(
            flops=2 * count * KIDS * 3 * feat * hidden,
            bytes_accessed=4 * count * KIDS * feat,
            transcendentals=0,
        ),
    )(*asked, wide, *packs)


def mirrored(value, count):
    result = 0
    while count > 1:
        result = result * 2 + value % 2
        value //= 2
        count //= 2
    return result


def far_first(count):
    return sorted(range(1, count), key=lambda step: (step < 2, step))


def shards(queries, node_table, beam, w_query, w_node, w_cross, bias_hidden, w_out):
    groups = lax.axis_size("blk")
    parts = lax.axis_size("hid")
    rows, width = beam.shape
    shard_rows = node_table.shape[0]
    binary = groups & (groups - 1) == 0 and parts & (parts - 1) == 0
    turns = groups // parts

    def hop_pairs(turn, back):
        pairs = []
        for b in range(groups):
            for h in range(parts):
                k = (mirrored(h, parts) if binary else h) * turns + turn
                if binary:
                    to = b ^ k
                else:
                    to = (b - k) % groups if not back else (b + k) % groups
                pairs.append((b * parts + h, to * parts + h))
        return pairs

    def hop(value, turn, back=False):
        return lax.ppermute(value, ("blk", "hid"), hop_pairs(turn, back))

    def across(value, step):
        pairs = [(h, h ^ step if binary else (h + step) % parts) for h in range(parts)]
        return lax.ppermute(value, "hid", pairs)

    digits = -(-(groups * shard_rows - 1).bit_length() // SHIFT)
    message, weights = pack(queries, beam, digits, (w_query, w_node, w_cross), w_out, bias_hidden)
    asked = []
    for turn in range(turns):
        asked.append(hop(message, turn))
    packs = [weights]
    for step in far_first(parts):
        packs.append(across(weights, step))
    scored = score_sources(asked, rows, shard_rows, widen(node_table), packs)
    total = sum(hop(s, turn, True).astype(jnp.float32) for turn, s in enumerate(scored))

    own = lax.axis_index("hid")
    piece = width // parts
    result = lax.dynamic_slice_in_dim(total, own * piece, piece, axis=0)
    for step in far_first(parts):
        peer = own ^ step if binary else (own + step) % parts
        sent = lax.dynamic_slice_in_dim(total, peer * piece, piece, axis=0)
        result = result + across(sent.astype(jnp.bfloat16), step).astype(jnp.float32)
    return result.T


def solution(mesh):
    in_specs = (
        P("blk", None),
        P("blk", None),
        P("blk", None),
        P(None, "hid"),
        P(None, "hid"),
        P(None, "hid"),
        P("hid"),
        P("hid"),
    )
    out_specs = P("blk", "hid")
    return jax.shard_map(shards, mesh=mesh, in_specs=in_specs, out_specs=out_specs, check_vma=False)
```

profile of v0, /device:TPU:1, one launch (start us, length us, event | category | flops | bytes accessed | tf_op | source)
XLA Modules:
  0.0 33.3 jit_solution(8971363864157088034)
XLA Ops:
  0.0 1.5 %shard_map.82 = (bf16[288,128]{1,0:T(8,128)(2,1)}, bf16[208,128]{1,0:T(8,128)(2,1)}) custom-call(s32[96,128]{1,0:T(8,128)} %refs_0_.1, bf16[96,128]{1,0:T(8,128)(2,1)} %refs_1_.1, bf16[64,128]{1,0:T(8,128)(2,1)} %bitcast.7, bf16[64,128]{1,0:T(8,128)(2,1)} %bitcast.8, bf16[64,128]{1,0:T(8,128)(2,1)} %bitcast.9, bf16[1,64]{1,0:T(2,128)(2,1)} %bitcast.10, ...), custom_call_target="tpu_custom_call" | custom-call | tf_op jit(solution)/shard_map/pallas_call | solution.py:64
  1.6 5.0 %collective-permute-start = (bf16[288,128]{1,0:T(8,128)(2,1)}, bf16[288,128]{1,0:T(8,128)(2,1)S(1)}, u32[]{:S(2)}, u32[]{:S(2)}) collective-permute-start(bf16[288,128]{1,0:T(8,128)(2,1)} %get-tuple-element.9), channel_id=1, source_target_pairs={{0,0},{1,17},{2,10},{3,27},{4,4},{5,21},{6,14},{7,31},{8,8},{9,25}... | collective-permute-start | bytes 221192 | tf_op jit(solution)/shard_map/ppermute | solution.py:360
  6.6 1.1 %collective-permute-start.1 = (bf16[288,128]{1,0:T(8,128)(2,1)}, bf16[288,128]{1,0:T(8,128)(2,1)S(1)}, u32[]{:S(2)}, u32[]{:S(2)}) collective-permute-start(bf16[288,128]{1,0:T(8,128)(2,1)} %get-tuple-element.9), channel_id=1, source_target_pairs={{0,4},{1,21},{2,14},{3,31},{4,0},{5,17},{6,10},{7,27},{8,12},{9,29... | collective-permute-start | bytes 221192 | tf_op jit(solution)/shard_map/ppermute | solution.py:360
  7.7 2.2 %collective-permute-start.2 = (bf16[208,128]{1,0:T(8,128)(2,1)}, bf16[208,128]{1,0:T(8,128)(2,1)S(1)}, u32[]{:S(2)}, u32[]{:S(2)}) collective-permute-start(bf16[208,128]{1,0:T(8,128)(2,1)} %get-tuple-element.10.refs_3_), channel_id=1, source_target_pairs={{0,2},{1,3},{2,0},{3,1},{4,6},{5,7},{6,4},{7,5},{8,10},{9,11},{10,... | collective-permute-start | bytes 159752 | tf_op jit(solution)/shard_map/ppermute | solution.py:364
  9.9 0.0 collective-permute-start.3
  9.9 0.4 %collective-permute-start.4 = (bf16[208,128]{1,0:T(8,128)(2,1)}, bf16[208,128]{1,0:T(8,128)(2,1)S(1)}, u32[]{:S(2)}, u32[]{:S(2)}) collective-permute-start(bf16[208,128]{1,0:T(8,128)(2,1)} %get-tuple-element.10.refs_3_), channel_id=1, source_target_pairs={{0,1},{1,0},{2,3},{3,2},{4,5},{5,4},{6,7},{7,6},{8,9},{9,8},{10,11... | collective-permute-start | bytes 159752 | tf_op jit(solution)/shard_map/ppermute | solution.py:364
  10.3 1.6 %copy-done = bf16[8192,128]{1,0:T(8,128)(2,1)S(1)} copy-done((bf16[8192,128]{1,0:T(8,128)(2,1)S(1)}, bf16[8192,128]{1,0:T(8,128)(2,1)}, u32[]{:S(2)}) %copy-start) | copy-done | bytes 2097176
  11.8 0.5 %shard_map.83.refs_2_ = f32[8192,128]{1,0:T(8,128)S(1)} custom-call(bf16[8192,128]{1,0:T(8,128)(2,1)S(1)} %copy-done), custom_call_target="tpu_custom_call" | custom-call | bytes 6291456 | tf_op jit(solution)/shard_map/pallas_call | solution.py:97
  12.4 0.0 collective-permute-done.2.refs_4_
  12.4 1.3 %collective-permute-done.3.refs_5_ = bf16[208,128]{1,0:T(8,128)(2,1)S(1)} collective-permute-done((bf16[208,128]{1,0:T(8,128)(2,1)}, bf16[208,128]{1,0:T(8,128)(2,1)S(1)}, u32[]{:S(2)}, u32[]{:S(2)}) %collective-permute-start.3) | collective-permute-done | bytes 53280 | tf_op jit(solution)/shard_map/ppermute | solution.py:364
  13.6 0.0 collective-permute-done.4.refs_6_
  13.6 0.0 collective-permute-done.refs_0_
  13.6 0.0 collective-permute-done.1.refs_1_
  13.6 3.8 %shard_map.84 = (bf16[128,96]{1,0:T(8,128)(2,1)S(1)}, bf16[128,96]{1,0:T(8,128)(2,1)S(1)}) custom-call(bf16[288,128]{1,0:T(8,128)(2,1)S(1)} %collective-permute-done.refs_0_, bf16[288,128]{1,0:T(8,128)(2,1)S(1)} %collective-permute-done.1.refs_1_, f32[8192,128]{1,0:T(8,128)S(1)} %shard_map.83.refs_2_, bf16[208,128]{1,0:T(8,128)(2,1)S(1)} %copy-done.1, ...), custom_call_target="tpu_custom_call" | custom-call | flops 603979776 | bytes 1572864 | tf_op jit(solution)/shard_map/pallas_call | solution.py:297
  17.5 3.7 %collective-permute-start.5 = (bf16[128,96]{1,0:T(8,128)(2,1)S(1)}, bf16[128,96]{1,0:T(8,128)(2,1)S(1)}, u32[]{:S(2)}, u32[]{:S(2)}) collective-permute-start(bf16[128,96]{1,0:T(8,128)(2,1)S(1)} %get-tuple-element.11), channel_id=1, source_target_pairs={{0,0},{1,17},{2,10},{3,27},{4,4},{5,21},{6,14},{7,31},{8,8},{9,25}... | collective-permute-start | bytes 73736 | tf_op jit(solution)/shard_map/ppermute | solution.py:360
  21.1 0.7 %collective-permute-start.6 = (bf16[128,96]{1,0:T(8,128)(2,1)S(1)}, bf16[128,96]{1,0:T(8,128)(2,1)S(1)}, u32[]{:S(2)}, u32[]{:S(2)}) collective-permute-start(bf16[128,96]{1,0:T(8,128)(2,1)S(1)} %get-tuple-element.12), channel_id=1, source_target_pairs={{0,4},{1,21},{2,14},{3,31},{4,0},{5,17},{6,10},{7,27},{8,12},{9,29... | collective-permute-start | bytes 73736 | tf_op jit(solution)/shard_map/ppermute | solution.py:360
  21.9 1.3 %collective-permute-done.5 = bf16[128,96]{1,0:T(8,128)(2,1)S(1)} collective-permute-done((bf16[128,96]{1,0:T(8,128)(2,1)S(1)}, bf16[128,96]{1,0:T(8,128)(2,1)S(1)}, u32[]{:S(2)}, u32[]{:S(2)}) %collective-permute-start.5) | collective-permute-done | bytes 24608 | tf_op jit(solution)/shard_map/ppermute | solution.py:360
  23.2 2.5 %collective-permute-done.6 = bf16[128,96]{1,0:T(8,128)(2,1)S(1)} collective-permute-done((bf16[128,96]{1,0:T(8,128)(2,1)S(1)}, bf16[128,96]{1,0:T(8,128)(2,1)S(1)}, u32[]{:S(2)}, u32[]{:S(2)}) %collective-permute-start.6) | collective-permute-done | bytes 24608 | tf_op jit(solution)/shard_map/ppermute | solution.py:360
  25.8 3.7 %collective-permute-start.7 = (bf16[32,96]{1,0:T(8,128)(2,1)S(1)}, bf16[32,96]{1,0:T(8,128)(2,1)S(1)}, u32[]{:S(2)}, u32[]{:S(2)}) collective-permute-start(bf16[32,96]{1,0:T(8,128)(2,1)S(1)} %get-tuple-element.13), channel_id=1, source_target_pairs={{0,2},{1,3},{2,0},{3,1},{4,6},{5,7},{6,4},{7,5},{8,10},{9,11},{10,... | collective-permute-start | bytes 18440 | tf_op jit(solution)/shard_map/ppermute | solution.py:364
  29.6 0.0 collective-permute-start.8
  29.6 0.5 %collective-permute-start.9 = (bf16[32,96]{1,0:T(8,128)(2,1)S(1)}, bf16[32,96]{1,0:T(8,128)(2,1)S(1)}, u32[]{:S(2)}, u32[]{:S(2)}) collective-permute-start(bf16[32,96]{1,0:T(8,128)(2,1)S(1)} %get-tuple-element.14), channel_id=1, source_target_pairs={{0,1},{1,0},{2,3},{3,2},{4,5},{5,4},{6,7},{7,6},{8,9},{9,8},{10,11... | collective-permute-start | bytes 18440 | tf_op jit(solution)/shard_map/ppermute | solution.py:364
  30.0 0.6 %collective-permute-done.7 = bf16[32,96]{1,0:T(8,128)(2,1)S(1)} collective-permute-done((bf16[32,96]{1,0:T(8,128)(2,1)S(1)}, bf16[32,96]{1,0:T(8,128)(2,1)S(1)}, u32[]{:S(2)}, u32[]{:S(2)}) %collective-permute-start.7) | collective-permute-done | bytes 6176 | tf_op jit(solution)/shard_map/ppermute | solution.py:364
  30.6 2.0 %collective-permute-done.8 = bf16[32,96]{1,0:T(8,128)(2,1)S(1)} collective-permute-done((bf16[32,96]{1,0:T(8,128)(2,1)S(1)}, bf16[32,96]{1,0:T(8,128)(2,1)S(1)}, u32[]{:S(2)}, u32[]{:S(2)}) %collective-permute-start.8) | collective-permute-done | bytes 6176 | tf_op jit(solution)/shard_map/ppermute | solution.py:364
  32.6 0.6 %add_bitcast_fusion = f32[96,32]{0,1:T(8,128)} fusion(bf16[32,96]{1,0:T(8,128)(2,1)S(1)} %collective-permute-done.9, bf16[32,96]{1,0:T(8,128)(2,1)S(1)} %collective-permute-done.8, bf16[32,96]{1,0:T(8,128)(2,1)S(1)} %collective-permute-done.7, f32[128,96]{1,0:T(8,128)S(1)} %convert_add_fusion, s32[]{:T(128)S(6)} %select_n.12), kind=kLoop, calls=%fused_computation.1 | loop fusion | flops 18432 | bytes 43012 | tf_op jit(solution)/shard_map/transpose | solution.py:384
  (6 shorter events, 0.0 us)
Async XLA Ops:
  1.6 12.1 %collective-permute-start = (bf16[288,128]{1,0:T(8,128)(2,1)}, bf16[288,128]{1,0:T(8,128)(2,1)S(1)}, u32[]{:S(2)}, u32[]{:S(2)}) collective-permute-start(bf16[288,128]{1,0:T(8,128)(2,1)} %get-tuple-element.9), channel_id=1, source_target_pairs={{0,0},{1,17},{2,10},{3,27},{4,4},{5,21},{6,14},{7,31},{8,8},{9,25}... | collective-permute-start | bytes 221192 | tf_op jit(solution)/shard_map/ppermute | solution.py:360
  6.6 7.0 %collective-permute-start.1 = (bf16[288,128]{1,0:T(8,128)(2,1)}, bf16[288,128]{1,0:T(8,128)(2,1)S(1)}, u32[]{:S(2)}, u32[]{:S(2)}) collective-permute-start(bf16[288,128]{1,0:T(8,128)(2,1)} %get-tuple-element.9), channel_id=1, source_target_pairs={{0,4},{1,21},{2,14},{3,31},{4,0},{5,17},{6,10},{7,27},{8,12},{9,29... | collective-permute-start | bytes 221192 | tf_op jit(solution)/shard_map/ppermute | solution.py:360
  7.7 4.7 %collective-permute-start.2 = (bf16[208,128]{1,0:T(8,128)(2,1)}, bf16[208,128]{1,0:T(8,128)(2,1)S(1)}, u32[]{:S(2)}, u32[]{:S(2)}) collective-permute-start(bf16[208,128]{1,0:T(8,128)(2,1)} %get-tuple-element.10.refs_3_), channel_id=1, source_target_pairs={{0,2},{1,3},{2,0},{3,1},{4,6},{5,7},{6,4},{7,5},{8,10},{9,11},{10,... | collective-permute-start | bytes 159752 | tf_op jit(solution)/shard_map/ppermute | solution.py:364
  9.9 3.8 %collective-permute-start.3 = (bf16[208,128]{1,0:T(8,128)(2,1)}, bf16[208,128]{1,0:T(8,128)(2,1)S(1)}, u32[]{:S(2)}, u32[]{:S(2)}) collective-permute-start(bf16[208,128]{1,0:T(8,128)(2,1)} %get-tuple-element.10.refs_3_), channel_id=1, source_target_pairs={{0,3},{1,2},{2,1},{3,0},{4,7},{5,6},{6,5},{7,4},{8,11},{9,10},{10,... | collective-permute-start | bytes 159752 | tf_op jit(solution)/shard_map/ppermute | solution.py:364
  9.9 3.8 %collective-permute-start.4 = (bf16[208,128]{1,0:T(8,128)(2,1)}, bf16[208,128]{1,0:T(8,128)(2,1)S(1)}, u32[]{:S(2)}, u32[]{:S(2)}) collective-permute-start(bf16[208,128]{1,0:T(8,128)(2,1)} %get-tuple-element.10.refs_3_), channel_id=1, source_target_pairs={{0,1},{1,0},{2,3},{3,2},{4,5},{5,4},{6,7},{7,6},{8,9},{9,8},{10,11... | collective-permute-start | bytes 159752 | tf_op jit(solution)/shard_map/ppermute | solution.py:364
  10.3 1.6 %copy-start = (bf16[8192,128]{1,0:T(8,128)(2,1)S(1)}, bf16[8192,128]{1,0:T(8,128)(2,1)}, u32[]{:S(2)}) copy-start(bf16[8192,128]{1,0:T(8,128)(2,1)} %table_ref.1) | copy-start | bytes 6291460
  11.8 1.8 %copy-start.1 = (bf16[208,128]{1,0:T(8,128)(2,1)S(1)}, bf16[208,128]{1,0:T(8,128)(2,1)}, u32[]{:S(2)}) copy-start(bf16[208,128]{1,0:T(8,128)(2,1)} %get-tuple-element.10.refs_3_) | copy-start | bytes 159748
  17.5 5.8 %collective-permute-start.5 = (bf16[128,96]{1,0:T(8,128)(2,1)S(1)}, bf16[128,96]{1,0:T(8,128)(2,1)S(1)}, u32[]{:S(2)}, u32[]{:S(2)}) collective-permute-start(bf16[128,96]{1,0:T(8,128)(2,1)S(1)} %get-tuple-element.11), channel_id=1, source_target_pairs={{0,0},{1,17},{2,10},{3,27},{4,4},{5,21},{6,14},{7,31},{8,8},{9,25}... | collective-permute-start | bytes 73736 | tf_op jit(solution)/shard_map/ppermute | solution.py:360
  21.1 4.6 %collective-permute-start.6 = (bf16[128,96]{1,0:T(8,128)(2,1)S(1)}, bf16[128,96]{1,0:T(8,128)(2,1)S(1)}, u32[]{:S(2)}, u32[]{:S(2)}) collective-permute-start(bf16[128,96]{1,0:T(8,128)(2,1)S(1)} %get-tuple-element.12), channel_id=1, source_target_pairs={{0,4},{1,21},{2,14},{3,31},{4,0},{5,17},{6,10},{7,27},{8,12},{9,29... | collective-permute-start | bytes 73736 | tf_op jit(solution)/shard_map/ppermute | solution.py:360
  25.8 4.8 %collective-permute-start.7 = (bf16[32,96]{1,0:T(8,128)(2,1)S(1)}, bf16[32,96]{1,0:T(8,128)(2,1)S(1)}, u32[]{:S(2)}, u32[]{:S(2)}) collective-permute-start(bf16[32,96]{1,0:T(8,128)(2,1)S(1)} %get-tuple-element.13), channel_id=1, source_target_pairs={{0,2},{1,3},{2,0},{3,1},{4,6},{5,7},{6,4},{7,5},{8,10},{9,11},{10,... | collective-permute-start | bytes 18440 | tf_op jit(solution)/shard_map/ppermute | solution.py:364
  29.6 3.1 %collective-permute-start.8 = (bf16[32,96]{1,0:T(8,128)(2,1)S(1)}, bf16[32,96]{1,0:T(8,128)(2,1)S(1)}, u32[]{:S(2)}, u32[]{:S(2)}) collective-permute-start(bf16[32,96]{1,0:T(8,128)(2,1)S(1)} %get-tuple-element.15), channel_id=1, source_target_pairs={{0,3},{1,2},{2,1},{3,0},{4,7},{5,6},{6,5},{7,4},{8,11},{9,10},{10,... | collective-permute-start | bytes 18440 | tf_op jit(solution)/shard_map/ppermute | solution.py:364
  29.6 3.1 %collective-permute-start.9 = (bf16[32,96]{1,0:T(8,128)(2,1)S(1)}, bf16[32,96]{1,0:T(8,128)(2,1)S(1)}, u32[]{:S(2)}, u32[]{:S(2)}) collective-permute-start(bf16[32,96]{1,0:T(8,128)(2,1)S(1)} %get-tuple-element.14), channel_id=1, source_target_pairs={{0,1},{1,0},{2,3},{3,2},{4,5},{5,4},{6,7},{7,6},{8,9},{9,8},{10,11... | collective-permute-start | bytes 18440 | tf_op jit(solution)/shard_map/ppermute | solution.py:364
where the time goes:
time: 33.5 us; the launch traced here: 33.3 us
  starting transfers between devices  17.3 us (52%)
  waiting for transfers between devices  7.75 us (23%)
  Pallas kernels  5.88 us (18%)
  local copies, waits for them, and re-layouts  1.61 us (5%)
  other arithmetic  0.62 us (2%)
    ppermute x4, starting transfers between devices, hop(): return lax.ppermute(value, ('blk', 'hid'), hop_pairs(turn, back))  10.5 us
    ppermute x6, starting transfers between devices, across(): return lax.ppermute(value, 'hid', pairs)  6.8 us
    ppermute x4, waiting for transfers between devices, hop(): return lax.ppermute(value, ('blk', 'hid'), hop_pairs(turn, back))  3.88 us
    ppermute x6, waiting for transfers between devices, across(): return lax.ppermute(value, 'hid', pairs)  3.86 us
    pallas_call x1, Pallas kernels, score_sources(): pl.pallas_call(functools.partial(score_kernel, shard_rows, digits, turns,...  3.83 us
    unnamed x4, local copies, waits for them, and re-layouts  1.59 us
    pallas_call x1, Pallas kernels, pack(): pl.pallas_call(functools.partial(pack_kernel, digits), in_specs=[pl.Block...  1.55 us
  transfers between devices with their start and end apart: 10, of which 5 were waited for; matrix products, arithmetic and copies ran while one was open for 0% of the time, Pallas kernels for 2%

commit v1 on v0

--- a/solution.py
+++ b/solution.py
@@ -12,12 +12,43 @@
 KIDS = 2 * SLOT
 READY = 2
 FIELD = 20
-SHIFT = 8
+SHIFT = 16
+BIAS = 127
+FRACTION = 7
+SIGN = 15
 LANES = 128
 SUBLANES = 8
 STATIC = 2
 
 VMEM = pl.BlockSpec(memory_space=pltpu.VMEM)
+
+
+def code_of(value):
+    size = jnp.abs(value)
+    kept = size >= 2.0 ** (1 - BIAS)
+    exponent = jnp.full(value.shape, BIAS, jnp.int32)
+    for k in (64, 32, 16, 8, 4, 2, 1):
+        low = size < 2.0 ** (1 - k)
+        size = jnp.where(low, size * 2.0**k, size)
+        exponent = jnp.where(low, exponent - k, exponent)
+    for k in (4, 2, 1):
+        high = size >= 2.0**k
+        size = jnp.where(high, size * 2.0**-k, size)
+        exponent = jnp.where(high, exponent + k, exponent)
+    fraction = ((size - 1.0) * 2.0**FRACTION).astype(jnp.int32)
+    code = (exponent << FRACTION) + fraction + jnp.where(value < 0, 1 << SIGN, 0)
+    return jnp.where(kept, code, 0)
+
+
+def value_of(code):
+    down = BIAS + FRACTION - ((code >> FRACTION) & (2 ** (SIGN - FRACTION) - 1))
+    value = ((code & (2**FRACTION - 1)) + 2**FRACTION).astype(jnp.float32)
+    for k in (64, 64, 32, 16, 8, 4, 2, 1):
+        take = down >= k
+        value = jnp.where(take, value * 2.0**-k, value)
+        down = jnp.where(take, down - k, down)
+    value = jnp.where((code >> SIGN) != 0, -value, value)
+    return jnp.where(code == 0, 0.0, value)
 
 
 def pack_kernel(digits, *refs):
@@ -38,10 +69,8 @@
     ids = beam_ref[...]
     for d in range(digits):
         digit = (ids >> (SHIFT * (digits - 1 - d))) & (2**SHIFT - 1)
-        message_ref[(d + 1) * rows : (d + 2) * rows, :] = digit.astype(jnp.float32).astype(
-            jnp.bfloat16
-        )
-    message_ref[0:rows, :] = query_ref[...]
+        message_ref[(d + 1) * rows : (d + 2) * rows, :] = digit.astype(jnp.uint16)
+    message_ref[0:rows, :] = code_of(query_ref[...].astype(jnp.float32)).astype(jnp.uint16)
     for i, weight in enumerate(weights):
         pack_ref[i * part : (i + 1) * part, :] = weight[...]
     tail = pack_ref.shape[0] - 3 * part
@@ -66,7 +95,7 @@
         in_specs=[pl.BlockSpec(memory_space=pltpu.HBM)] * len(given),
         out_specs=(VMEM, VMEM),
         out_shape=(
-            jax.ShapeDtypeStruct(((digits + 1) * rows, width), jnp.bfloat16),
+            jax.ShapeDtypeStruct(((digits + 1) * rows, width), jnp.uint16),
             jax.ShapeDtypeStruct((3 * part + 16, width), jnp.bfloat16),
         ),
         scratch_shapes=[pltpu.VMEM(x.shape, x.dtype) for x in given]
@@ -131,10 +160,10 @@
     tiles = rows // tile_queries
     limit = width // 2 // SLOT
 
-    ids = jnp.concatenate([a[rows : 2 * rows, :] for a in asked], axis=0).astype(jnp.int32)
+    ids = jnp.concatenate([a[rows : 2 * rows, :].astype(jnp.int32) for a in asked], axis=0)
     for d in range(2, digits + 1):
-        digit = jnp.concatenate([a[d * rows : (d + 1) * rows, :] for a in asked], axis=0)
-        ids = (ids << SHIFT) + digit.astype(jnp.int32)
+        digit = [a[d * rows : (d + 1) * rows, :].astype(jnp.int32) for a in asked]
+        ids = (ids << SHIFT) + jnp.concatenate(digit, axis=0)
     local = ids - lax.axis_index("blk") * shard_rows
     owned = (local >= 0) & (local < shard_rows)
     even = owned & ((local & 1) == 0)
@@ -183,8 +212,10 @@
     out_row = jnp.concatenate([e[0:1, 0:part] for e in ends], axis=1)
     bias = jnp.concatenate([e[1:2, 0:part] for e in ends], axis=1)
     out_row_ref[...] = jnp.broadcast_to(out_row, out_row_ref.shape)
-    queries = jnp.concatenate([a[0:rows, :] for a in asked], axis=0)
-    query_ref[...] = queries.astype(jnp.float32)
+    codes = jnp.concatenate([a[0:rows, :].astype(jnp.int32) for a in asked], axis=0)
+    exact = value_of(codes)
+    query_ref[...] = exact
+    queries = exact.astype(jnp.bfloat16)
     start_ref[...] = (
         jnp.dot(queries, stacked[0].T, preferred_element_type=jnp.float32) + bias
     )

time: 33.5 us -> 35 us (1.045)
  starting transfers between devices: 17.3 us -> 18.9 us
    ppermute x6, starting transfers between devices: 6.8 us -> 8.23 us  [across(): return lax.ppermute(value, 'hid', pairs)]
    ppermute x6, waiting for transfers between devices: 3.86 us -> 2.61 us  [across(): return lax.ppermute(value, 'hid', pairs)]
    ppermute x4, waiting for transfers between devices: 3.88 us -> 4.86 us  [hop(): return lax.ppermute(value, ('blk', 'hid'), hop_pairs(turn, back))]
  transfers between devices with their start and end apart: 10 -> 10, of which waited for: 5 -> 5; matrix products, arithmetic and copies ran while one was open for 0% -> 0% of each run, Pallas kernels for 2% -> 1%
where the time goes in v1:
time: 35 us; the launch traced here: 34.7 us
  starting transfers between devices  18.9 us (54%)
  waiting for transfers between devices  7.47 us (21%)
  Pallas kernels  5.99 us (17%)
  local copies, waits for them, and re-layouts  1.61 us (5%)
  other arithmetic  0.62 us (2%)
    ppermute x4, starting transfers between devices, hop(): return lax.ppermute(value, ('blk', 'hid'), hop_pairs(turn, back))  10.7 us
    ppermute x6, starting transfers between devices, across(): return lax.ppermute(value, 'hid', pairs)  8.23 us
    ppermute x4, waiting for transfers between devices, hop(): return lax.ppermute(value, ('blk', 'hid'), hop_pairs(turn, back))  4.86 us
    pallas_call x1, Pallas kernels, score_sources(): pl.pallas_call(functools.partial(score_kernel, shard_rows, digits, turns,...  3.87 us
    ppermute x6, waiting for transfers between devices, across(): return lax.ppermute(value, 'hid', pairs)  2.61 us
    pallas_call x1, Pallas kernels, pack(): pl.pallas_call(functools.partial(pack_kernel, digits), in_specs=[pl.Block...  1.62 us
    unnamed x4, local copies, waits for them, and re-layouts  1.59 us
  transfers between devices with their start and end apart: 10, of which 5 were waited for; matrix products, arithmetic and copies ran while one was open for 0% of the time, Pallas kernels for 1%

profile of v1, /device:TPU:1, one launch (start us, length us, event | category | flops | bytes accessed | tf_op | source)
XLA Modules:
  0.0 34.7 jit_solution(7055720630268607336)
XLA Ops:
  0.0 1.6 %shard_map.82 = (u16[192,128]{1,0:T(8,128)(2,1)}, bf16[208,128]{1,0:T(8,128)(2,1)}) custom-call(s32[96,128]{1,0:T(8,128)} %refs_0_.1, bf16[96,128]{1,0:T(8,128)(2,1)} %refs_1_.1, bf16[64,128]{1,0:T(8,128)(2,1)} %bitcast.7, bf16[64,128]{1,0:T(8,128)(2,1)} %bitcast.8, bf16[64,128]{1,0:T(8,128)(2,1)} %bitcast.9, bf16[1,64]{1,0:T(2,128)(2,1)} %bitcast.10, ...), custom_call_target="tpu_custom_call" | custom-call | tf_op jit(solution)/shard_map/pallas_call | solution.py:93
  1.6 2.1 %collective-permute-start.2 = (bf16[208,128]{1,0:T(8,128)(2,1)}, bf16[208,128]{1,0:T(8,128)(2,1)S(1)}, u32[]{:S(2)}, u32[]{:S(2)}) collective-permute-start(bf16[208,128]{1,0:T(8,128)(2,1)} %get-tuple-element.10.refs_3_), channel_id=1, source_target_pairs={{0,2},{1,3},{2,0},{3,1},{4,6},{5,7},{6,4},{7,5},{8,10},{9,11},{10,... | collective-permute-start | bytes 159752 | tf_op jit(solution)/shard_map/ppermute | solution.py:395
  3.7 0.6 %collective-permute-start.3 = (bf16[208,128]{1,0:T(8,128)(2,1)}, bf16[208,128]{1,0:T(8,128)(2,1)S(1)}, u32[]{:S(2)}, u32[]{:S(2)}) collective-permute-start(bf16[208,128]{1,0:T(8,128)(2,1)} %get-tuple-element.10.refs_3_), channel_id=1, source_target_pairs={{0,3},{1,2},{2,1},{3,0},{4,7},{5,6},{6,5},{7,4},{8,11},{9,10},{10,... | collective-permute-start | bytes 159752 | tf_op jit(solution)/shard_map/ppermute | solution.py:395
  4.4 0.3 collective-permute-start.4
  4.7 4.3 %collective-permute-start = (u16[192,128]{1,0:T(8,128)(2,1)}, u16[192,128]{1,0:T(8,128)(2,1)S(1)}, u32[]{:S(2)}, u32[]{:S(2)}) collective-permute-start(u16[192,128]{1,0:T(8,128)(2,1)} %get-tuple-element.9), channel_id=1, source_target_pairs={{0,0},{1,17},{2,10},{3,27},{4,4},{5,21},{6,14},{7,31},{8,8},{9,25}... | collective-permute-start | bytes 147464 | tf_op jit(solution)/shard_map/ppermute | solution.py:391
  9.0 1.1 %collective-permute-start.1 = (u16[192,128]{1,0:T(8,128)(2,1)}, u16[192,128]{1,0:T(8,128)(2,1)S(1)}, u32[]{:S(2)}, u32[]{:S(2)}) collective-permute-start(u16[192,128]{1,0:T(8,128)(2,1)} %get-tuple-element.9), channel_id=1, source_target_pairs={{0,4},{1,21},{2,14},{3,31},{4,0},{5,17},{6,10},{7,27},{8,12},{9,29... | collective-permute-start | bytes 147464 | tf_op jit(solution)/shard_map/ppermute | solution.py:391
  10.1 1.6 %copy-done = bf16[8192,128]{1,0:T(8,128)(2,1)S(1)} copy-done((bf16[8192,128]{1,0:T(8,128)(2,1)S(1)}, bf16[8192,128]{1,0:T(8,128)(2,1)}, u32[]{:S(2)}) %copy-start) | copy-done | bytes 2097176
  11.7 0.5 %shard_map.83.refs_2_ = f32[8192,128]{1,0:T(8,128)S(1)} custom-call(bf16[8192,128]{1,0:T(8,128)(2,1)S(1)} %copy-done), custom_call_target="tpu_custom_call" | custom-call | bytes 6291456 | tf_op jit(solution)/shard_map/pallas_call | solution.py:126
  12.2 0.0 collective-permute-done.refs_0_
  12.2 1.8 %collective-permute-done.1.refs_1_ = u16[192,128]{1,0:T(8,128)(2,1)S(1)} collective-permute-done((u16[192,128]{1,0:T(8,128)(2,1)}, u16[192,128]{1,0:T(8,128)(2,1)S(1)}, u32[]{:S(2)}, u32[]{:S(2)}) %collective-permute-start.1) | collective-permute-done | bytes 49184 | tf_op jit(solution)/shard_map/ppermute | solution.py:391
  14.0 0.0 collective-permute-done.2.refs_4_
  14.0 0.0 collective-permute-done.3.refs_5_
  14.1 0.0 collective-permute-done.4.refs_6_
  14.1 3.9 %shard_map.84 = (bf16[128,96]{1,0:T(8,128)(2,1)S(1)}, bf16[128,96]{1,0:T(8,128)(2,1)S(1)}) custom-call(u16[192,128]{1,0:T(8,128)(2,1)S(1)} %collective-permute-done.refs_0_, u16[192,128]{1,0:T(8,128)(2,1)S(1)} %collective-permute-done.1.refs_1_, f32[8192,128]{1,0:T(8,128)S(1)} %shard_map.83.refs_2_, bf16[208,128]{1,0:T(8,128)(2,1)S(1)} %copy-done.1, ...), custom_call_target="tpu_custom_call" | custom-call | flops 603979776 | bytes 1572864 | tf_op jit(solution)/shard_map/pallas_call | solution.py:328
  17.9 3.7 %collective-permute-start.5 = (bf16[128,96]{1,0:T(8,128)(2,1)S(1)}, bf16[128,96]{1,0:T(8,128)(2,1)S(1)}, u32[]{:S(2)}, u32[]{:S(2)}) collective-permute-start(bf16[128,96]{1,0:T(8,128)(2,1)S(1)} %get-tuple-element.11), channel_id=1, source_target_pairs={{0,0},{1,17},{2,10},{3,27},{4,4},{5,21},{6,14},{7,31},{8,8},{9,25}... | collective-permute-start | bytes 73736 | tf_op jit(solution)/shard_map/ppermute | solution.py:391
  21.7 1.6 %collective-permute-start.6 = (bf16[128,96]{1,0:T(8,128)(2,1)S(1)}, bf16[128,96]{1,0:T(8,128)(2,1)S(1)}, u32[]{:S(2)}, u32[]{:S(2)}) collective-permute-start(bf16[128,96]{1,0:T(8,128)(2,1)S(1)} %get-tuple-element.12), channel_id=1, source_target_pairs={{0,4},{1,21},{2,14},{3,31},{4,0},{5,17},{6,10},{7,27},{8,12},{9,29... | collective-permute-start | bytes 73736 | tf_op jit(solution)/shard_map/ppermute | solution.py:391
  23.2 0.3 collective-permute-done.5
  23.5 2.8 %collective-permute-done.6 = bf16[128,96]{1,0:T(8,128)(2,1)S(1)} collective-permute-done((bf16[128,96]{1,0:T(8,128)(2,1)S(1)}, bf16[128,96]{1,0:T(8,128)(2,1)S(1)}, u32[]{:S(2)}, u32[]{:S(2)}) %collective-permute-start.6) | collective-permute-done | bytes 24608 | tf_op jit(solution)/shard_map/ppermute | solution.py:391
  26.3 4.7 %collective-permute-start.7 = (bf16[32,96]{1,0:T(8,128)(2,1)S(1)}, bf16[32,96]{1,0:T(8,128)(2,1)S(1)}, u32[]{:S(2)}, u32[]{:S(2)}) collective-permute-start(bf16[32,96]{1,0:T(8,128)(2,1)S(1)} %get-tuple-element.13), channel_id=1, source_target_pairs={{0,2},{1,3},{2,0},{3,1},{4,6},{5,7},{6,4},{7,5},{8,10},{9,11},{10,... | collective-permute-start | bytes 18440 | tf_op jit(solution)/shard_map/ppermute | solution.py:395
  31.0 0.0 collective-permute-start.8
  31.0 0.5 %collective-permute-start.9 = (bf16[32,96]{1,0:T(8,128)(2,1)S(1)}, bf16[32,96]{1,0:T(8,128)(2,1)S(1)}, u32[]{:S(2)}, u32[]{:S(2)}) collective-permute-start(bf16[32,96]{1,0:T(8,128)(2,1)S(1)} %get-tuple-element.14), channel_id=1, source_target_pairs={{0,1},{1,0},{2,3},{3,2},{4,5},{5,4},{6,7},{7,6},{8,9},{9,8},{10,11... | collective-permute-start | bytes 18440 | tf_op jit(solution)/shard_map/ppermute | solution.py:395
  31.5 0.6 %collective-permute-done.7 = bf16[32,96]{1,0:T(8,128)(2,1)S(1)} collective-permute-done((bf16[32,96]{1,0:T(8,128)(2,1)S(1)}, bf16[32,96]{1,0:T(8,128)(2,1)S(1)}, u32[]{:S(2)}, u32[]{:S(2)}) %collective-permute-start.7) | collective-permute-done | bytes 6176 | tf_op jit(solution)/shard_map/ppermute | solution.py:395
  32.1 2.0 %collective-permute-done.8 = bf16[32,96]{1,0:T(8,128)(2,1)S(1)} collective-permute-done((bf16[32,96]{1,0:T(8,128)(2,1)S(1)}, bf16[32,96]{1,0:T(8,128)(2,1)S(1)}, u32[]{:S(2)}, u32[]{:S(2)}) %collective-permute-start.8) | collective-permute-done | bytes 6176 | tf_op jit(solution)/shard_map/ppermute | solution.py:395
  34.1 0.6 %add_bitcast_fusion = f32[96,32]{0,1:T(8,128)} fusion(bf16[32,96]{1,0:T(8,128)(2,1)S(1)} %collective-permute-done.9, bf16[32,96]{1,0:T(8,128)(2,1)S(1)} %collective-permute-done.8, bf16[32,96]{1,0:T(8,128)(2,1)S(1)} %collective-permute-done.7, f32[128,96]{1,0:T(8,128)S(1)} %convert_add_fusion, s32[]{:T(128)S(6)} %select_n.12), kind=kLoop, calls=%fused_computation.1 | loop fusion | flops 18432 | bytes 43012 | tf_op jit(solution)/shard_map/transpose | solution.py:415
  (6 shorter events, 0.0 us)
Async XLA Ops:
  1.6 12.4 %collective-permute-start.2 = (bf16[208,128]{1,0:T(8,128)(2,1)}, bf16[208,128]{1,0:T(8,128)(2,1)S(1)}, u32[]{:S(2)}, u32[]{:S(2)}) collective-permute-start(bf16[208,128]{1,0:T(8,128)(2,1)} %get-tuple-element.10.refs_3_), channel_id=1, source_target_pairs={{0,2},{1,3},{2,0},{3,1},{4,6},{5,7},{6,4},{7,5},{8,10},{9,11},{10,... | collective-permute-start | bytes 159752 | tf_op jit(solution)/shard_map/ppermute | solution.py:395
  3.7 10.3 %collective-permute-start.3 = (bf16[208,128]{1,0:T(8,128)(2,1)}, bf16[208,128]{1,0:T(8,128)(2,1)S(1)}, u32[]{:S(2)}, u32[]{:S(2)}) collective-permute-start(bf16[208,128]{1,0:T(8,128)(2,1)} %get-tuple-element.10.refs_3_), channel_id=1, source_target_pairs={{0,3},{1,2},{2,1},{3,0},{4,7},{5,6},{6,5},{7,4},{8,11},{9,10},{10,... | collective-permute-start | bytes 159752 | tf_op jit(solution)/shard_map/ppermute | solution.py:395
  4.4 9.7 %collective-permute-start.4 = (bf16[208,128]{1,0:T(8,128)(2,1)}, bf16[208,128]{1,0:T(8,128)(2,1)S(1)}, u32[]{:S(2)}, u32[]{:S(2)}) collective-permute-start(bf16[208,128]{1,0:T(8,128)(2,1)} %get-tuple-element.10.refs_3_), channel_id=1, source_target_pairs={{0,1},{1,0},{2,3},{3,2},{4,5},{5,4},{6,7},{7,6},{8,9},{9,8},{10,11... | collective-permute-start | bytes 159752 | tf_op jit(solution)/shard_map/ppermute | solution.py:395
  4.7 7.5 %collective-permute-start = (u16[192,128]{1,0:T(8,128)(2,1)}, u16[192,128]{1,0:T(8,128)(2,1)S(1)}, u32[]{:S(2)}, u32[]{:S(2)}) collective-permute-start(u16[192,128]{1,0:T(8,128)(2,1)} %get-tuple-element.9), channel_id=1, source_target_pairs={{0,0},{1,17},{2,10},{3,27},{4,4},{5,21},{6,14},{7,31},{8,8},{9,25}... | collective-permute-start | bytes 147464 | tf_op jit(solution)/shard_map/ppermute | solution.py:391
  9.0 5.0 %collective-permute-start.1 = (u16[192,128]{1,0:T(8,128)(2,1)}, u16[192,128]{1,0:T(8,128)(2,1)S(1)}, u32[]{:S(2)}, u32[]{:S(2)}) collective-permute-start(u16[192,128]{1,0:T(8,128)(2,1)} %get-tuple-element.9), channel_id=1, source_target_pairs={{0,4},{1,21},{2,14},{3,31},{4,0},{5,17},{6,10},{7,27},{8,12},{9,29... | collective-permute-start | bytes 147464 | tf_op jit(solution)/shard_map/ppermute | solution.py:391
  10.1 1.6 %copy-start = (bf16[8192,128]{1,0:T(8,128)(2,1)S(1)}, bf16[8192,128]{1,0:T(8,128)(2,1)}, u32[]{:S(2)}) copy-start(bf16[8192,128]{1,0:T(8,128)(2,1)} %table_ref.1) | copy-start | bytes 6291460
  11.7 2.4 %copy-start.1 = (bf16[208,128]{1,0:T(8,128)(2,1)S(1)}, bf16[208,128]{1,0:T(8,128)(2,1)}, u32[]{:S(2)}) copy-start(bf16[208,128]{1,0:T(8,128)(2,1)} %get-tuple-element.10.refs_3_) | copy-start | bytes 159748
  17.9 5.6 %collective-permute-start.5 = (bf16[128,96]{1,0:T(8,128)(2,1)S(1)}, bf16[128,96]{1,0:T(8,128)(2,1)S(1)}, u32[]{:S(2)}, u32[]{:S(2)}) collective-permute-start(bf16[128,96]{1,0:T(8,128)(2,1)S(1)} %get-tuple-element.11), channel_id=1, source_target_pairs={{0,0},{1,17},{2,10},{3,27},{4,4},{5,21},{6,14},{7,31},{8,8},{9,25}... | collective-permute-start | bytes 73736 | tf_op jit(solution)/shard_map/ppermute | solution.py:391
  21.7 4.6 %collective-permute-start.6 = (bf16[128,96]{1,0:T(8,128)(2,1)S(1)}, bf16[128,96]{1,0:T(8,128)(2,1)S(1)}, u32[]{:S(2)}, u32[]{:S(2)}) collective-permute-start(bf16[128,96]{1,0:T(8,128)(2,1)S(1)} %get-tuple-element.12), channel_id=1, source_target_pairs={{0,4},{1,21},{2,14},{3,31},{4,0},{5,17},{6,10},{7,27},{8,12},{9,29... | collective-permute-start | bytes 73736 | tf_op jit(solution)/shard_map/ppermute | solution.py:391
  26.3 5.8 %collective-permute-start.7 = (bf16[32,96]{1,0:T(8,128)(2,1)S(1)}, bf16[32,96]{1,0:T(8,128)(2,1)S(1)}, u32[]{:S(2)}, u32[]{:S(2)}) collective-permute-start(bf16[32,96]{1,0:T(8,128)(2,1)S(1)} %get-tuple-element.13), channel_id=1, source_target_pairs={{0,2},{1,3},{2,0},{3,1},{4,6},{5,7},{6,4},{7,5},{8,10},{9,11},{10,... | collective-permute-start | bytes 18440 | tf_op jit(solution)/shard_map/ppermute | solution.py:395
  31.0 3.1 %collective-permute-start.8 = (bf16[32,96]{1,0:T(8,128)(2,1)S(1)}, bf16[32,96]{1,0:T(8,128)(2,1)S(1)}, u32[]{:S(2)}, u32[]{:S(2)}) collective-permute-start(bf16[32,96]{1,0:T(8,128)(2,1)S(1)} %get-tuple-element.15), channel_id=1, source_target_pairs={{0,3},{1,2},{2,1},{3,0},{4,7},{5,6},{6,5},{7,4},{8,11},{9,10},{10,... | collective-permute-start | bytes 18440 | tf_op jit(solution)/shard_map/ppermute | solution.py:395
  31.0 3.1 %collective-permute-start.9 = (bf16[32,96]{1,0:T(8,128)(2,1)S(1)}, bf16[32,96]{1,0:T(8,128)(2,1)S(1)}, u32[]{:S(2)}, u32[]{:S(2)}) collective-permute-start(bf16[32,96]{1,0:T(8,128)(2,1)S(1)} %get-tuple-element.14), channel_id=1, source_target_pairs={{0,1},{1,0},{2,3},{3,2},{4,5},{5,4},{6,7},{7,6},{8,9},{9,8},{10,11... | collective-permute-start | bytes 18440 | tf_op jit(solution)/shard_map/ppermute | solution.py:395
